TPU v7x, 32 devices: a whole 2x2x4 slice. The times are simulated.
32 devices in a mesh: blk: 16 (over z, y, core), rep: 2 (over x).
Axes of the slice: x: 2, y: 2, z: 4, core: 2. Of those that a mesh axis runs over, the one named last changes fastest.
Arguments:
- features: bfloat16 [16384, 256], P('blk'), may hold values from -6 to 6
- weight_self: bfloat16 [256, 256], replicated, may hold values from -0.375 to 0.375
- weight_neighbor: bfloat16 [256, 256], replicated, may hold values from -0.375 to 0.375
- bias_vector: float32 [256], replicated, may hold values from -3 to 3
- tile_row: int32 [16, 16, 64], P('blk', 'rep'), may hold values from 0 to 7
- tile_column: int32 [16, 16, 64], P('blk', 'rep'), may hold values from 0 to 7
- tile_value: int32 [16, 16, 64], P('blk', 'rep'), may hold values from 0 to 127
- tile_count: int32 [16, 16], P('blk', 'rep'), may hold values from 16 to 64
- tile_table: bfloat16 [4096, 128, 128], P(('blk', 'rep')), may hold values from -0.0625 to 0.0625
- cotangent: bfloat16 [16384, 256], P('blk'), may hold values from -6 to 6
Outputs:
- activations: bfloat16 [16384, 256], P('blk')
- grad_features: bfloat16 [16384, 256], P('blk')
- grad_weight_self: float32 [256, 256], replicated
- grad_weight_neighbor: float32 [256, 256], replicated
- grad_bias: float32 [256], replicated
All inputs are finite; a program needn't handle non-finite values.
Results may differ from a plain program's by a relative error of at most 0.025.
Values may be sent and summed in bfloat16 or wider, within the bound.
A program may use at most 64 MiB of HBM per device.

v0:
```python
import jax
import jax.numpy as jnp
from jax import lax
from jax.sharding import PartitionSpec as P


def from_behind(array, axis, by):
    length = lax.axis_size(axis)
    return lax.ppermute(array, axis, [(i, (i + by) % length) for i in range(length)])


def gather_terms(tile_table, source_blocks, row_pick, column_pick, value_pick, live_count, forward):
    slot_count = row_pick.shape[0]
    block_count = source_blocks.shape[0]
    is_live = jnp.arange(slot_count) < live_count
    tile_values = jnp.take(tile_table, value_pick, axis=0)
    if forward:
        picked = jnp.take(source_blocks, column_pick, axis=0)
        products = jnp.einsum(
            "kab,kbf->kaf", tile_values, picked, preferred_element_type=jnp.float32
        )
        target_pick = row_pick
    else:
        picked = jnp.take(source_blocks, row_pick, axis=0)
        products = jnp.einsum(
            "kab,kaf->kbf", tile_values, picked, preferred_element_type=jnp.float32
        )
        target_pick = column_pick
    placing = (
        (target_pick[:, None] == jnp.arange(block_count)[None, :]) & is_live[:, None]
    ).astype(jnp.float32)
    return jnp.einsum("kr,kaf->raf", placing, products, preferred_element_type=jnp.float32)


def on_device(
    features,
    weight_self,
    weight_neighbor,
    bias_vector,
    tile_row,
    tile_column,
    tile_value,
    tile_count,
    tile_table,
    cotangent,
):
    cycle_length = lax.axis_size("blk")
    replicas = lax.axis_size("rep")
    step_count = cycle_length // replicas
    rep_bits = replicas.bit_length() - 1
    replica = lax.axis_index("rep")
    row_total, feature_width = features.shape
    tile_size = tile_table.shape[1]
    block_count = row_total // tile_size
    row_lists = tile_row[0]
    column_lists = tile_column[0]
    value_lists = tile_value[0]
    live_counts = tile_count[0]

    def step_term(source_blocks, offset, forward):
        return gather_terms(
            tile_table,
            source_blocks,
            lax.dynamic_index_in_dim(row_lists, offset, 0, False),
            lax.dynamic_index_in_dim(column_lists, offset, 0, False),
            lax.dynamic_index_in_dim(value_lists, offset, 0, False),
            lax.dynamic_index_in_dim(live_counts, offset, 0, False),
            forward,
        )

    def shape_blocks(matrix):
        return matrix.reshape(block_count, tile_size, feature_width)

    feature_panel = features
    for bit_index in range(rep_bits):
        shifted = from_behind(feature_panel, "blk", step_count << bit_index)
        feature_panel = jnp.where(replica // (1 << bit_index) % 2 == 1, shifted, feature_panel)
    partial_sum = step_term(shape_blocks(feature_panel), 0, True)

    def cycle_step(offset, carry):
        panel_now, running = carry
        panel_now = from_behind(panel_now, "blk", 1)
        return (panel_now, running + step_term(shape_blocks(panel_now), offset, True))

    feature_panel, partial_sum = lax.fori_loop(
        1, step_count, cycle_step, (feature_panel, partial_sum)
    )
    partial_sum = partial_sum.reshape(row_total, feature_width)
    aggregate = lax.psum(partial_sum, "rep")
    aggregate_b = aggregate.astype(jnp.bfloat16)
    before = jnp.dot(features, weight_self, preferred_element_type=jnp.float32)
    before = (
        before
        + jnp.dot(aggregate_b, weight_neighbor, preferred_element_type=jnp.float32)
        + bias_vector
    )
    sigmoid_pre = jax.nn.sigmoid(before)
    output_rows = (before * sigmoid_pre).astype(jnp.bfloat16)
    derivative = sigmoid_pre * (1.0 + before * (1.0 - sigmoid_pre))
    grad_pre = (cotangent.astype(jnp.float32) * derivative).astype(jnp.bfloat16)
    contract_rows = (((0,), (0,)), ((), ()))
    contract_columns = (((1,), (1,)), ((), ()))
    grad_self = lax.dot_general(
        features, grad_pre, contract_rows, preferred_element_type=jnp.float32
    )
    grad_neighbor = lax.dot_general(
        aggregate_b, grad_pre, contract_rows, preferred_element_type=jnp.float32
    )
    grad_offset = jnp.sum(grad_pre.astype(jnp.float32), axis=0)
    self_term = lax.dot_general(
        grad_pre, weight_self, contract_columns, preferred_element_type=jnp.float32
    )
    sent_back = lax.dot_general(
        grad_pre, weight_neighbor, contract_columns, preferred_element_type=jnp.float32
    ).astype(jnp.bfloat16)
    grad_self, grad_neighbor, grad_offset = (
        lax.psum(grad_self.astype(jnp.bfloat16), "blk").astype(jnp.float32),
        lax.psum(grad_neighbor.astype(jnp.bfloat16), "blk").astype(jnp.float32),
        lax.psum(grad_offset.astype(jnp.bfloat16), "blk").astype(jnp.float32),
    )
    back_blocks = shape_blocks(sent_back)
    pushed = step_term(back_blocks, step_count - 1, False)

    def push_step(offset, running):
        running = from_behind(running, "blk", -1)
        return running + step_term(back_blocks, step_count - 1 - offset, False)

    pushed = lax.fori_loop(1, step_count, push_step, pushed)
    for bit_index in range(rep_bits):
        shifted = from_behind(
            pushed.astype(jnp.bfloat16), "blk", -(step_count << bit_index)
        ).astype(pushed.dtype)
        pushed = jnp.where(replica // (1 << bit_index) % 2 == 1, shifted, pushed)
    pushed = pushed.reshape(row_total, feature_width)
    neighbor_term = lax.psum(pushed.astype(jnp.bfloat16), "rep").astype(jnp.float32)
    grad_features = (self_term + neighbor_term).astype(jnp.bfloat16)
    return (output_rows, grad_features, grad_self, grad_neighbor, grad_offset)


def solution(mesh):
    placed = (
        P("blk", None),
        P(),
        P(),
        P(),
        P("blk", "rep", None),
        P("blk", "rep", None),
        P("blk", "rep", None),
        P("blk", "rep"),
        P(("blk", "rep"), None, None),
        P("blk", None),
    )
    return jax.shard_map(
        on_device,
        mesh=mesh,
        in_specs=placed,
        out_specs=(P("blk", None), P("blk", None), P(), P(), P()),
        check_vma=False,
    )
```

profile of v0, /device:TPU:0, one launch (start us, length us, event | category | flops | bytes accessed | tf_op | source)
XLA Modules:
  0.0 519.6 jit_solution(10854658101296210277)
XLA Ops:
  7.2 4.1 collective-permute-start.2
  19.4 4.4 gather_fusion.6
  25.8 9.0 %collective-permute-done.2 = bf16[1024,256]{1,0:T(8,128)(2,1)} collective-permute-done((bf16[1024,256]{1,0:T(8,128)(2,1)}, bf16[1024,256]{1,0:T(8,128)(2,1)}, u32[]{:S(2)}, u32[]{:S(2)}) %collective-permute-start.2) | collective-permute-done | bytes 524320 | tf_op jit(solution)/shard_map/ppermute | solution.py:9
  37.7 3.5 fusion.48
  41.2 3.4 fusion.44
  44.6 147.8 %while.32 = (s32[]{:T(128)}, bf16[1024,256]{1,0:T(8,128)(2,1)S(1)}, f32[8,128,256]{2,0,1:T(8,128)}, s32[8,64]{1,0:T(8,128)}, s32[8]{0:T(128)S(1)}, /*index=5*/s3...) while((s32[]{:T(128)}, bf16[1024,256]{1,0:T(8,128)(2,1)S(1)}, ...), condition=%wide.region_1.4_spmd, body=%wide.region_0.3_spmd.sunk | while | flops 573837120 | bytes 40906124 | solution.py:85
  50.4 5.5 %collective-permute-done = bf16[1024,256]{1,0:T(8,128)(2,1)S(1)} collective-permute-done((bf16[1024,256]{1,0:T(8,128)(2,1)S(1)}, bf16[1024,256]{1,0:T(8,128)(2,1)S(1)}, u32[]{:S(2)}, u32[]{:S(2)}) %collective-permute-start) | collective-permute-done | bytes 524320 | tf_op jit(solution)/shard_map/while/body/eval_jaxpr/ppermute | solution.py:9
  58.7 3.6 fusion.110
  71.5 5.5 %collective-permute-done = bf16[1024,256]{1,0:T(8,128)(2,1)S(1)} collective-permute-done((bf16[1024,256]{1,0:T(8,128)(2,1)S(1)}, bf16[1024,256]{1,0:T(8,128)(2,1)S(1)}, u32[]{:S(2)}, u32[]{:S(2)}) %collective-permute-start) | collective-permute-done | bytes 524320 | tf_op jit(solution)/shard_map/while/body/eval_jaxpr/ppermute | solution.py:9
  79.8 3.6 fusion.110
  92.6 5.5 %collective-permute-done = bf16[1024,256]{1,0:T(8,128)(2,1)S(1)} collective-permute-done((bf16[1024,256]{1,0:T(8,128)(2,1)S(1)}, bf16[1024,256]{1,0:T(8,128)(2,1)S(1)}, u32[]{:S(2)}, u32[]{:S(2)}) %collective-permute-start) | collective-permute-done | bytes 524320 | tf_op jit(solution)/shard_map/while/body/eval_jaxpr/ppermute | solution.py:9
  100.9 3.6 fusion.110
  113.7 5.5 %collective-permute-done = bf16[1024,256]{1,0:T(8,128)(2,1)S(1)} collective-permute-done((bf16[1024,256]{1,0:T(8,128)(2,1)S(1)}, bf16[1024,256]{1,0:T(8,128)(2,1)S(1)}, u32[]{:S(2)}, u32[]{:S(2)}) %collective-permute-start) | collective-permute-done | bytes 524320 | tf_op jit(solution)/shard_map/while/body/eval_jaxpr/ppermute | solution.py:9
  122.0 3.6 fusion.110
  134.9 5.5 %collective-permute-done = bf16[1024,256]{1,0:T(8,128)(2,1)S(1)} collective-permute-done((bf16[1024,256]{1,0:T(8,128)(2,1)S(1)}, bf16[1024,256]{1,0:T(8,128)(2,1)S(1)}, u32[]{:S(2)}, u32[]{:S(2)}) %collective-permute-start) | collective-permute-done | bytes 524320 | tf_op jit(solution)/shard_map/while/body/eval_jaxpr/ppermute | solution.py:9
  143.1 3.6 fusion.110
  156.0 5.5 %collective-permute-done = bf16[1024,256]{1,0:T(8,128)(2,1)S(1)} collective-permute-done((bf16[1024,256]{1,0:T(8,128)(2,1)S(1)}, bf16[1024,256]{1,0:T(8,128)(2,1)S(1)}, u32[]{:S(2)}, u32[]{:S(2)}) %collective-permute-start) | collective-permute-done | bytes 524320 | tf_op jit(solution)/shard_map/while/body/eval_jaxpr/ppermute | solution.py:9
  164.2 3.6 fusion.110
  177.1 5.5 %collective-permute-done = bf16[1024,256]{1,0:T(8,128)(2,1)S(1)} collective-permute-done((bf16[1024,256]{1,0:T(8,128)(2,1)S(1)}, bf16[1024,256]{1,0:T(8,128)(2,1)S(1)}, u32[]{:S(2)}, u32[]{:S(2)}) %collective-permute-start) | collective-permute-done | bytes 524320 | tf_op jit(solution)/shard_map/while/body/eval_jaxpr/ppermute | solution.py:9
  185.4 3.6 fusion.110
  194.0 23.9 %all-reduce.8 = bf16[1024,256]{1,0:T(8,128)(2,1)S(1)} all-reduce(f32[1024,256]{1,0:T(8,128)S(1)} %bitcast.97), channel_id=1, replica_groups=mesh['blk'=16,'rep'=2] {'rep'}, use_global_device_ids=true, to_apply=%region_2.5 | all-reduce | flops 262144 | bytes 1572864 | tf_op jit(solution)/shard_map/psum | solution.py:89
  224.2 4.1 fusion.46
  228.3 3.3 fusion.42
  231.6 148.3 %while.33 = (s32[]{:T(128)}, f32[8,128,256]{2,0,1:T(8,128)}, s32[8,64]{1,0:T(8,128)}, s32[8]{0:T(128)S(1)}, s32[8,64]{1,0:T(8,128)}, /*index=5*/bf16[128,128,128...) while((s32[]{:T(128)}, f32[8,128,256]{2,0,1:T(8,128)}, ...), condition=%wide.region_4.7_spmd, body=%wide.region_3.6_spmd.sunk | while | flops 573837120 | bytes 33566048 | solution.py:128
  240.3 4.1 fusion.117
  244.4 4.6 fusion.119
  249.0 4.5 collective-permute-start.1
  262.1 4.1 fusion.117
  266.2 4.6 fusion.119
  270.8 4.5 collective-permute-start.1
  283.9 4.1 fusion.117
  288.0 4.6 fusion.119
  292.6 4.5 collective-permute-start.1
  305.8 4.1 fusion.117
  309.9 4.6 fusion.119
  314.5 4.5 collective-permute-start.1
  327.6 4.1 fusion.117
  331.7 4.6 fusion.119
  336.3 4.5 collective-permute-start.1
  349.4 4.1 fusion.117
  353.5 4.6 fusion.119
  358.1 4.5 collective-permute-start.1
  371.2 4.1 fusion.117
  375.4 4.6 fusion.119
  385.5 6.5 %collective-permute-done.3 = bf16[8,128,256]{2,0,1:T(8,128)(2,1)S(1)} collective-permute-done((bf16[8,128,256]{2,0,1:T(8,128)(2,1)S(1)}, bf16[8,128,256]{2,0,1:T(8,128)(2,1)S(1)}, u32[]{:S(2)}, u32[]{:S(2)}) %collective-permute-start.3) | collective-permute-done | bytes 524320 | tf_op jit(solution)/shard_map/ppermute | solution.py:9
  394.3 36.1 %psum.39 = bf16[256]{0:T(256)(128)(2,1)S(1)} all-reduce(bf16[256]{0:T(256)(128)(2,1)S(1)} %get-tuple-element.457), channel_id=1, replica_groups=mesh['blk'=16,'rep'=2] {'blk'}, use_global_device_ids=true, to_apply=%region_9.12 | all-reduce | flops 256 | bytes 1024 | tf_op jit(solution)/shard_map/psum | solution.py:119
  430.9 47.6 %all-reduce.7.cloned.1.call-done = (bf16[256,256]{0,1:T(8,128)(2,1)}, bf16[256,256]{1,0:T(8,128)(2,1)}) async-done(((bf16[256,256]{0,1:T(8,128)(2,1)}, bf16[256,256]{1,0:T(8,128)(2,1)}), (bf16[256,256]{0,1:T(8,128)(2,1)}, bf16[256,256]{1,0:T(8,128)(2,1)})) %all-reduce.7.cloned.1.call-update) | async-done | bytes 262160 | tf_op jit(solution)/shard_map/psum | solution.py:117
  481.9 28.7 %all-reduce.5.cloned.1.call-done = bf16[1024,256]{1,0:T(8,128)(2,1)} async-done(((bf16[1024,256]{1,0:T(8,128)(2,1)}), bf16[1024,256]{1,0:T(8,128)(2,1)}) %all-reduce.5.cloned.1.call-update) | async-done | bytes 524304 | tf_op jit(solution)/shard_map/psum | solution.py:135
  (219 shorter events, 178.5 us)
Async XLA Ops:
  7.2 210.7 %copy-start = (bf16[256,256]{1,0:T(8,128)(2,1)S(1)}, bf16[256,256]{1,0:T(8,128)(2,1)}, u32[]{:S(2)}) copy-start(bf16[256,256]{1,0:T(8,128)(2,1)} %param.20) | copy-start | bytes 393220
  7.2 471.4 %all-reduce.7.cloned.1.call-start = ((), (), s32[]{:S(2)}) async-start(), calls=%async_computation.1 | async-start | bytes 524288 | tf_op jit(solution)/shard_map/psum | solution.py:117
  7.2 27.6 %collective-permute-start.2 = (bf16[1024,256]{1,0:T(8,128)(2,1)}, bf16[1024,256]{1,0:T(8,128)(2,1)}, u32[]{:S(2)}, u32[]{:S(2)}) collective-permute-start(bf16[1024,256]{1,0:T(8,128)(2,1)} %param.18), channel_id=1, source_target_pairs={{0,16},{2,18},{4,20},{6,22},{8,24},{10,26},{12,28},{14,30},{16,0},... | collective-permute-start | bytes 1572872 | tf_op jit(solution)/shard_map/ppermute | solution.py:9
  16.2 8.3 %copy-start.4 = (bf16[1024,256]{1,0:T(8,128)(2,1)S(1)}, bf16[1024,256]{1,0:T(8,128)(2,1)}, u32[]{:S(2)}) copy-start(bf16[1024,256]{1,0:T(8,128)(2,1)} %param.18) | copy-start | bytes 1572868
  16.2 8.3 %copy-start.7 = (bf16[256,256]{1,0:T(8,128)(2,1)S(1)}, bf16[256,256]{1,0:T(8,128)(2,1)}, u32[]{:S(2)}) copy-start(bf16[256,256]{1,0:T(8,128)(2,1)} %param.19) | copy-start | bytes 393220
  41.2 3.4 copy-start.8
  44.6 173.3 %copy-start.9 = (f32[256]{0:T(256)S(1)}, f32[256]{0:T(256)}, u32[]{:S(2)}) copy-start(f32[256]{0:T(256)} %param.21) | copy-start | bytes 3076
  44.6 11.3 %collective-permute-start = (bf16[1024,256]{1,0:T(8,128)(2,1)S(1)}, bf16[1024,256]{1,0:T(8,128)(2,1)S(1)}, u32[]{:S(2)}, u32[]{:S(2)}) collective-permute-start(bf16[1024,256]{1,0:T(8,128)(2,1)S(1)} %get-tuple-element.605), channel_id=1, source_target_pairs={{0,2},{2,4},{4,6},{6,8},{8,10},{10,12},{12,14},{14,16},{16,18},{18... | collective-permute-start | bytes 1572872 | tf_op jit(solution)/shard_map/while/body/eval_jaxpr/ppermute | solution.py:9
  58.7 3.6 copy-start.1
  64.7 1.0 copy-start.2
  65.7 11.3 %collective-permute-start = (bf16[1024,256]{1,0:T(8,128)(2,1)S(1)}, bf16[1024,256]{1,0:T(8,128)(2,1)S(1)}, u32[]{:S(2)}, u32[]{:S(2)}) collective-permute-start(bf16[1024,256]{1,0:T(8,128)(2,1)S(1)} %get-tuple-element.605), channel_id=1, source_target_pairs={{0,2},{2,4},{4,6},{6,8},{8,10},{10,12},{12,14},{14,16},{16,18},{18... | collective-permute-start | bytes 1572872 | tf_op jit(solution)/shard_map/while/body/eval_jaxpr/ppermute | solution.py:9
  79.8 3.6 copy-start.1
  85.8 1.0 copy-start.2
  86.8 11.3 %collective-permute-start = (bf16[1024,256]{1,0:T(8,128)(2,1)S(1)}, bf16[1024,256]{1,0:T(8,128)(2,1)S(1)}, u32[]{:S(2)}, u32[]{:S(2)}) collective-permute-start(bf16[1024,256]{1,0:T(8,128)(2,1)S(1)} %get-tuple-element.605), channel_id=1, source_target_pairs={{0,2},{2,4},{4,6},{6,8},{8,10},{10,12},{12,14},{14,16},{16,18},{18... | collective-permute-start | bytes 1572872 | tf_op jit(solution)/shard_map/while/body/eval_jaxpr/ppermute | solution.py:9
  100.9 3.6 copy-start.1
  106.9 1.0 copy-start.2
  107.9 11.3 %collective-permute-start = (bf16[1024,256]{1,0:T(8,128)(2,1)S(1)}, bf16[1024,256]{1,0:T(8,128)(2,1)S(1)}, u32[]{:S(2)}, u32[]{:S(2)}) collective-permute-start(bf16[1024,256]{1,0:T(8,128)(2,1)S(1)} %get-tuple-element.605), channel_id=1, source_target_pairs={{0,2},{2,4},{4,6},{6,8},{8,10},{10,12},{12,14},{14,16},{16,18},{18... | collective-permute-start | bytes 1572872 | tf_op jit(solution)/shard_map/while/body/eval_jaxpr/ppermute | solution.py:9
  122.0 3.6 copy-start.1
  128.0 1.0 copy-start.2
  129.0 11.3 %collective-permute-start = (bf16[1024,256]{1,0:T(8,128)(2,1)S(1)}, bf16[1024,256]{1,0:T(8,128)(2,1)S(1)}, u32[]{:S(2)}, u32[]{:S(2)}) collective-permute-start(bf16[1024,256]{1,0:T(8,128)(2,1)S(1)} %get-tuple-element.605), channel_id=1, source_target_pairs={{0,2},{2,4},{4,6},{6,8},{8,10},{10,12},{12,14},{14,16},{16,18},{18... | collective-permute-start | bytes 1572872 | tf_op jit(solution)/shard_map/while/body/eval_jaxpr/ppermute | solution.py:9
  143.1 3.6 copy-start.1
  149.1 1.0 copy-start.2
  150.2 11.3 %collective-permute-start = (bf16[1024,256]{1,0:T(8,128)(2,1)S(1)}, bf16[1024,256]{1,0:T(8,128)(2,1)S(1)}, u32[]{:S(2)}, u32[]{:S(2)}) collective-permute-start(bf16[1024,256]{1,0:T(8,128)(2,1)S(1)} %get-tuple-element.605), channel_id=1, source_target_pairs={{0,2},{2,4},{4,6},{6,8},{8,10},{10,12},{12,14},{14,16},{16,18},{18... | collective-permute-start | bytes 1572872 | tf_op jit(solution)/shard_map/while/body/eval_jaxpr/ppermute | solution.py:9
  164.2 3.6 copy-start.1
  170.2 1.0 copy-start.2
  171.3 11.3 %collective-permute-start = (bf16[1024,256]{1,0:T(8,128)(2,1)S(1)}, bf16[1024,256]{1,0:T(8,128)(2,1)S(1)}, u32[]{:S(2)}, u32[]{:S(2)}) collective-permute-start(bf16[1024,256]{1,0:T(8,128)(2,1)S(1)} %get-tuple-element.605), channel_id=1, source_target_pairs={{0,2},{2,4},{4,6},{6,8},{8,10},{10,12},{12,14},{14,16},{16,18},{18... | collective-permute-start | bytes 1572872 | tf_op jit(solution)/shard_map/while/body/eval_jaxpr/ppermute | solution.py:9
  185.4 3.6 copy-start.1
  191.3 1.0 copy-start.2
  194.0 26.7 %copy-start.5 = (bf16[1024,256]{1,0:T(8,128)(2,1)S(1)}, bf16[1024,256]{1,0:T(8,128)(2,1)}, u32[]{:S(2)}) copy-start(bf16[1024,256]{1,0:T(8,128)(2,1)} %param.27) | copy-start | bytes 1572868
  217.9 3.5 copy-start.6
  221.4 2.8 copy-start.3
  231.6 12.7 %collective-permute-start.1 = (f32[8,128,256]{2,0,1:T(8,128)}, f32[8,128,256]{2,0,1:T(8,128)}, u32[]{:S(2)}, u32[]{:S(2)}) collective-permute-start(f32[8,128,256]{2,0,1:T(8,128)} %get-tuple-element.639), channel_id=1, source_target_pairs={{0,30},{2,0},{4,2},{6,4},{8,6},{10,8},{12,10},{14,12},{16,14},{18,... | collective-permute-start | bytes 3145736 | tf_op jit(solution)/shard_map/while/body/eval_jaxpr/ppermute | solution.py:9
  249.0 17.2 %collective-permute-start.1 = (f32[8,128,256]{2,0,1:T(8,128)}, f32[8,128,256]{2,0,1:T(8,128)}, u32[]{:S(2)}, u32[]{:S(2)}) collective-permute-start(f32[8,128,256]{2,0,1:T(8,128)} %get-tuple-element.639), channel_id=1, source_target_pairs={{0,30},{2,0},{4,2},{6,4},{8,6},{10,8},{12,10},{14,12},{16,14},{18,... | collective-permute-start | bytes 3145736 | tf_op jit(solution)/shard_map/while/body/eval_jaxpr/ppermute | solution.py:9
  270.8 17.2 %collective-permute-start.1 = (f32[8,128,256]{2,0,1:T(8,128)}, f32[8,128,256]{2,0,1:T(8,128)}, u32[]{:S(2)}, u32[]{:S(2)}) collective-permute-start(f32[8,128,256]{2,0,1:T(8,128)} %get-tuple-element.639), channel_id=1, source_target_pairs={{0,30},{2,0},{4,2},{6,4},{8,6},{10,8},{12,10},{14,12},{16,14},{18,... | collective-permute-start | bytes 3145736 | tf_op jit(solution)/shard_map/while/body/eval_jaxpr/ppermute | solution.py:9
  292.6 17.2 %collective-permute-start.1 = (f32[8,128,256]{2,0,1:T(8,128)}, f32[8,128,256]{2,0,1:T(8,128)}, u32[]{:S(2)}, u32[]{:S(2)}) collective-permute-start(f32[8,128,256]{2,0,1:T(8,128)} %get-tuple-element.639), channel_id=1, source_target_pairs={{0,30},{2,0},{4,2},{6,4},{8,6},{10,8},{12,10},{14,12},{16,14},{18,... | collective-permute-start | bytes 3145736 | tf_op jit(solution)/shard_map/while/body/eval_jaxpr/ppermute | solution.py:9
  314.5 17.2 %collective-permute-start.1 = (f32[8,128,256]{2,0,1:T(8,128)}, f32[8,128,256]{2,0,1:T(8,128)}, u32[]{:S(2)}, u32[]{:S(2)}) collective-permute-start(f32[8,128,256]{2,0,1:T(8,128)} %get-tuple-element.639), channel_id=1, source_target_pairs={{0,30},{2,0},{4,2},{6,4},{8,6},{10,8},{12,10},{14,12},{16,14},{18,... | collective-permute-start | bytes 3145736 | tf_op jit(solution)/shard_map/while/body/eval_jaxpr/ppermute | solution.py:9
  336.3 17.2 %collective-permute-start.1 = (f32[8,128,256]{2,0,1:T(8,128)}, f32[8,128,256]{2,0,1:T(8,128)}, u32[]{:S(2)}, u32[]{:S(2)}) collective-permute-start(f32[8,128,256]{2,0,1:T(8,128)} %get-tuple-element.639), channel_id=1, source_target_pairs={{0,30},{2,0},{4,2},{6,4},{8,6},{10,8},{12,10},{14,12},{16,14},{18,... | collective-permute-start | bytes 3145736 | tf_op jit(solution)/shard_map/while/body/eval_jaxpr/ppermute | solution.py:9
  358.1 17.2 %collective-permute-start.1 = (f32[8,128,256]{2,0,1:T(8,128)}, f32[8,128,256]{2,0,1:T(8,128)}, u32[]{:S(2)}, u32[]{:S(2)}) collective-permute-start(f32[8,128,256]{2,0,1:T(8,128)} %get-tuple-element.639), channel_id=1, source_target_pairs={{0,30},{2,0},{4,2},{6,4},{8,6},{10,8},{12,10},{14,12},{16,14},{18,... | collective-permute-start | bytes 3145736 | tf_op jit(solution)/shard_map/while/body/eval_jaxpr/ppermute | solution.py:9
  381.2 10.8 %collective-permute-start.3 = (bf16[8,128,256]{2,0,1:T(8,128)(2,1)S(1)}, bf16[8,128,256]{2,0,1:T(8,128)(2,1)S(1)}, u32[]{:S(2)}, u32[]{:S(2)}) collective-permute-start(bf16[8,128,256]{2,0,1:T(8,128)(2,1)S(1)} %convert_element_type.66), channel_id=1, source_target_pairs={{0,16},{2,18},{4,20},{6,22},{8,24},{10,26},{12,28},{14,30},{16,0},... | collective-permute-start | bytes 1572872 | tf_op jit(solution)/shard_map/ppermute | solution.py:9
  385.4 125.2 %all-reduce.5.cloned.1.call-start = ((), (), s32[]{:S(2)}) async-start(), calls=%async_computation | async-start | bytes 1048576 | tf_op jit(solution)/shard_map/psum | solution.py:135
Sparse Core Ops, SparseCore 0:
  385.6 92.9 all-reduce.6
  481.4 29.1 all-reduce.4
where the time goes:
time: 522 us; the launch traced here: 520 us
  waiting for transfers between devices  130 us (25%)
  local copies, waits for them, and re-layouts  128 us (25%)
  matrix products  127 us (24%)
  blocking collectives  60 us (11%)
  starting transfers between devices  31.5 us (6%)
  other arithmetic  27.4 us (5%)
  between operations  14.2 us (3%)
    dot_general x16, matrix products, gather_terms(): jnp.einsum('kr,kaf->raf', placing, products, preferred_element_type=jnp.f...  55.3 us
    ppermute x16, waiting for transfers between devices, from_behind(): lax.ppermute(array, axis, [(i, (i + by) % length) for i in range(length)])  54 us
    gather x16, local copies, waits for them, and re-layouts, gather_terms(): tile_values = jnp.take(tile_table, value_pick, axis=0)  51.5 us
    psum x1, waiting for transfers between devices, on_device(): lax.psum(grad_self.astype(jnp.bfloat16), 'blk').astype(jnp.float32)  47.6 us
    psum x1, blocking collectives, on_device(): lax.psum(grad_offset.astype(jnp.bfloat16), 'blk').astype(jnp.float32)  36.1 us
    dot_general x8, matrix products, gather_terms(): jnp.einsum('kab,kaf->kbf', tile_values, picked, preferred_element_type=jn...  32.8 us
    ppermute x16, starting transfers between devices, from_behind(): lax.ppermute(array, axis, [(i, (i + by) % length) for i in range(length)])  31.5 us
    dot_general x8, matrix products, gather_terms(): jnp.einsum('kab,kbf->kaf', tile_values, picked, preferred_element_type=jn...  28.7 us
  transfers between devices with their start and end apart: 18, of which 11 were waited for; matrix products, arithmetic and copies ran while one was open for 30% of the time, Pallas kernels for 0%

commit v1 on v0

--- a/solution.py
+++ b/solution.py
@@ -114,7 +114,7 @@
         grad_pre, weight_neighbor, contract_columns, preferred_element_type=jnp.float32
     ).astype(jnp.bfloat16)
     grad_self, grad_neighbor, grad_offset = (
-        lax.psum(grad_self.astype(jnp.bfloat16), "blk").astype(jnp.float32),
+        jnp.sum(lax.all_gather(grad_self.astype(jnp.bfloat16), "blk"), axis=0).astype(jnp.float32),
         lax.psum(grad_neighbor.astype(jnp.bfloat16), "blk").astype(jnp.float32),
         lax.psum(grad_offset.astype(jnp.bfloat16), "blk").astype(jnp.float32),
     )

time: 522 us -> 564 us (1.080)
  waiting for transfers between devices: 130 us -> 171 us
    all_gather x0 -> x1, waiting for transfers between devices: none -> 41.6 us  [on_device(): lax.all_gather(grad_self.astype(jnp.bfloat16), 'blk')]
    psum x1, waiting for transfers between devices: 47.6 us -> 42 us  [on_device(): lax.psum(grad_neighbor.astype(jnp.bfloat16), 'blk').astype(jnp.float32)]
  transfers between devices with their start and end apart: 18 -> 19, of which waited for: 11 -> 12; matrix products, arithmetic and copies ran while one was open for 30% -> 27% of each run, Pallas kernels for 0% -> 0%
where the time goes in v1:
time: 564 us; the launch traced here: 561 us
  waiting for transfers between devices  171 us (30%)
  local copies, waits for them, and re-layouts  129 us (23%)
  matrix products  126 us (22%)
  blocking collectives  59.9 us (11%)
  starting transfers between devices  31.6 us (6%)
  other arithmetic  28.6 us (5%)
  between operations  14 us (2%)
    ppermute x16, waiting for transfers between devices, from_behind(): lax.ppermute(array, axis, [(i, (i + by) % length) for i in range(length)])  56 us
    dot_general x16, matrix products, gather_terms(): jnp.einsum('kr,kaf->raf', placing, products, preferred_element_type=jnp.f...  55.3 us
    gather x16, local copies, waits for them, and re-layouts, gather_terms(): tile_values = jnp.take(tile_table, value_pick, axis=0)  51.5 us
    psum x1, waiting for transfers between devices, on_device(): lax.psum(grad_neighbor.astype(jnp.bfloat16), 'blk').astype(jnp.float32)  42 us
    all_gather x1, waiting for transfers between devices, on_device(): lax.all_gather(grad_self.astype(jnp.bfloat16), 'blk')  41.6 us
    psum x1, blocking collectives, on_device(): lax.psum(grad_offset.astype(jnp.bfloat16), 'blk').astype(jnp.float32)  36 us
    dot_general x8, matrix products, gather_terms(): jnp.einsum('kab,kaf->kbf', tile_values, picked, preferred_element_type=jn...  32.8 us
    psum x1, waiting for transfers between devices, on_device(): lax.psum(pushed.astype(jnp.bfloat16), 'rep').astype(jnp.float32)  31.5 us
  transfers between devices with their start and end apart: 19, of which 12 were waited for; matrix products, arithmetic and copies ran while one was open for 27% of the time, Pallas kernels for 0%

profile of v1, /device:TPU:0, one launch (start us, length us, event | category | flops | bytes accessed | tf_op | source)
XLA Modules:
  0.0 561.1 jit_solution(6382895859318732071)
XLA Ops:
  7.2 4.1 collective-permute-start.2
  19.4 4.3 gather_fusion.6
  25.8 9.0 %collective-permute-done.2 = bf16[1024,256]{1,0:T(8,128)(2,1)} collective-permute-done((bf16[1024,256]{1,0:T(8,128)(2,1)}, bf16[1024,256]{1,0:T(8,128)(2,1)}, u32[]{:S(2)}, u32[]{:S(2)}) %collective-permute-start.2) | collective-permute-done | bytes 524320 | tf_op jit(solution)/shard_map/ppermute | solution.py:9
  37.7 3.5 fusion.48
  41.2 3.3 fusion.44
  44.5 147.5 %while.32 = (s32[]{:T(128)}, bf16[1024,256]{1,0:T(8,128)(2,1)S(1)}, f32[8,128,256]{2,0,1:T(8,128)}, s32[8,64]{1,0:T(8,128)}, s32[8]{0:T(128)S(1)}, /*index=5*/s3...) while((s32[]{:T(128)}, bf16[1024,256]{1,0:T(8,128)(2,1)S(1)}, ...), condition=%wide.region_1.4_spmd, body=%wide.region_0.3_spmd.sunk | while | flops 573837120 | bytes 40906124 | solution.py:85
  50.4 5.5 collective-permute-done
  58.6 3.6 fusion.110
  71.4 5.5 collective-permute-done
  79.7 3.6 fusion.110
  92.5 5.5 collective-permute-done
  100.8 3.6 fusion.110
  113.6 5.5 collective-permute-done
  121.8 3.6 fusion.110
  134.7 5.5 collective-permute-done
  142.9 3.6 fusion.110
  155.7 5.5 collective-permute-done
  164.0 3.6 fusion.110
  176.8 5.5 collective-permute-done
  185.1 3.6 fusion.110
  193.7 23.9 %all-reduce.7 = bf16[1024,256]{1,0:T(8,128)(2,1)S(1)} all-reduce(f32[1024,256]{1,0:T(8,128)S(1)} %bitcast.102), channel_id=1, replica_groups=mesh['blk'=16,'rep'=2] {'rep'}, use_global_device_ids=true, to_apply=%region_2.5 | all-reduce | flops 262144 | bytes 1572864 | tf_op jit(solution)/shard_map/psum | solution.py:89
  223.9 4.1 fusion.46
  231.3 148.2 %while.33 = (s32[]{:T(128)}, f32[8,128,256]{2,0,1:T(8,128)}, s32[8,64]{1,0:T(8,128)}, s32[8]{0:T(128)S(1)}, s32[8,64]{1,0:T(8,128)}, /*index=5*/bf16[128,128,128...) while((s32[]{:T(128)}, f32[8,128,256]{2,0,1:T(8,128)}, ...), condition=%wide.region_4.7_spmd, body=%wide.region_3.6_spmd.sunk | while | flops 573837120 | bytes 33566048 | solution.py:128
  239.9 4.1 fusion.117
  244.0 4.6 fusion.119
  248.6 4.5 collective-permute-start.1
  261.7 4.1 fusion.117
  265.8 4.6 fusion.119
  270.4 4.5 collective-permute-start.1
  283.5 4.1 fusion.117
  287.6 4.6 fusion.119
  292.2 4.5 collective-permute-start.1
  305.3 4.1 fusion.117
  309.5 4.6 fusion.119
  314.1 4.5 collective-permute-start.1
  327.2 4.1 fusion.117
  331.3 4.6 fusion.119
  335.9 4.5 collective-permute-start.1
  349.0 4.1 fusion.117
  353.1 4.6 fusion.119
  357.7 4.6 collective-permute-start.1
  370.8 4.1 fusion.117
  374.9 4.6 fusion.119
  383.0 8.5 %collective-permute-done.3 = bf16[8,128,256]{2,0,1:T(8,128)(2,1)S(1)} collective-permute-done((bf16[8,128,256]{2,0,1:T(8,128)(2,1)S(1)}, bf16[8,128,256]{2,0,1:T(8,128)(2,1)S(1)}, u32[]{:S(2)}, u32[]{:S(2)}) %collective-permute-start.3) | collective-permute-done | bytes 524320 | tf_op jit(solution)/shard_map/ppermute | solution.py:9
  394.9 36.0 %psum.31 = bf16[256]{0:T(256)(128)(2,1)S(1)} all-reduce(bf16[256]{0:T(256)(128)(2,1)S(1)} %get-tuple-element.450), channel_id=1, replica_groups=mesh['blk'=16,'rep'=2] {'blk'}, use_global_device_ids=true, to_apply=%region_9.12 | all-reduce | flops 256 | bytes 1024 | tf_op jit(solution)/shard_map/psum | solution.py:119
  431.5 42.0 %all-reduce.6.cloned.1.call-done = bf16[256,256]{1,0:T(8,128)(2,1)} async-done(((bf16[256,256]{1,0:T(8,128)(2,1)}), bf16[256,256]{1,0:T(8,128)(2,1)}) %all-reduce.6.cloned.1.call-update) | async-done | bytes 131088 | tf_op jit(solution)/shard_map/psum | solution.py:118
  475.1 31.5 %all-reduce.4.cloned.1.call-done = bf16[1024,256]{1,0:T(8,128)(2,1)} async-done(((bf16[1024,256]{1,0:T(8,128)(2,1)}), bf16[1024,256]{1,0:T(8,128)(2,1)}) %all-reduce.4.cloned.1.call-update) | async-done | bytes 524304 | tf_op jit(solution)/shard_map/psum | solution.py:135
  508.7 41.6 %all-gather.3.cloned.1.call-done = bf16[4096,256]{0,1:T(8,128)(2,1)} async-done(((bf16[256,256]{0,1:T(8,128)(2,1)}), bf16[4096,256]{0,1:T(8,128)(2,1)}) %all-gather.3.cloned.1.call-update) | async-done | bytes 2097168 | tf_op jit(solution)/shard_map/all_gather | solution.py:117
  (226 shorter events, 183.0 us)
Async XLA Ops:
  7.2 210.4 %copy-start = (bf16[256,256]{1,0:T(8,128)(2,1)S(1)}, bf16[256,256]{1,0:T(8,128)(2,1)}, u32[]{:S(2)}) copy-start(bf16[256,256]{1,0:T(8,128)(2,1)} %param.20) | copy-start | bytes 393220
  7.2 466.3 %all-reduce.6.cloned.1.call-start = ((), (), s32[]{:S(2)}) async-start(), calls=%async_computation.1 | async-start | bytes 262144 | tf_op jit(solution)/shard_map/psum | solution.py:118
  7.2 27.6 %collective-permute-start.2 = (bf16[1024,256]{1,0:T(8,128)(2,1)}, bf16[1024,256]{1,0:T(8,128)(2,1)}, u32[]{:S(2)}, u32[]{:S(2)}) collective-permute-start(bf16[1024,256]{1,0:T(8,128)(2,1)} %param.18), channel_id=1, source_target_pairs={{0,16},{2,18},{4,20},{6,22},{8,24},{10,26},{12,28},{14,30},{16,0},... | collective-permute-start | bytes 1572872 | tf_op jit(solution)/shard_map/ppermute | solution.py:9
  16.2 8.3 %copy-start.4 = (bf16[1024,256]{1,0:T(8,128)(2,1)S(1)}, bf16[1024,256]{1,0:T(8,128)(2,1)}, u32[]{:S(2)}) copy-start(bf16[1024,256]{1,0:T(8,128)(2,1)} %param.18) | copy-start | bytes 1572868
  16.2 8.3 %copy-start.8 = (bf16[256,256]{1,0:T(8,128)(2,1)S(1)}, bf16[256,256]{1,0:T(8,128)(2,1)}, u32[]{:S(2)}) copy-start(bf16[256,256]{1,0:T(8,128)(2,1)} %param.19) | copy-start | bytes 393220
  41.2 3.4 copy-start.9
  44.5 173.1 %copy-start.10 = (f32[256]{0:T(256)S(1)}, f32[256]{0:T(256)}, u32[]{:S(2)}) copy-start(f32[256]{0:T(256)} %param.21) | copy-start | bytes 3076
  44.5 11.3 %collective-permute-start = (bf16[1024,256]{1,0:T(8,128)(2,1)S(1)}, bf16[1024,256]{1,0:T(8,128)(2,1)S(1)}, u32[]{:S(2)}, u32[]{:S(2)}) collective-permute-start(bf16[1024,256]{1,0:T(8,128)(2,1)S(1)} %get-tuple-element.598), channel_id=1, source_target_pairs={{0,2},{2,4},{4,6},{6,8},{8,10},{10,12},{12,14},{14,16},{16,18},{18... | collective-permute-start | bytes 1572872 | tf_op jit(solution)/shard_map/while/body/eval_jaxpr/ppermute | solution.py:9
  58.6 3.6 copy-start.1
  64.6 1.0 copy-start.2
  65.6 11.3 %collective-permute-start = (bf16[1024,256]{1,0:T(8,128)(2,1)S(1)}, bf16[1024,256]{1,0:T(8,128)(2,1)S(1)}, u32[]{:S(2)}, u32[]{:S(2)}) collective-permute-start(bf16[1024,256]{1,0:T(8,128)(2,1)S(1)} %get-tuple-element.598), channel_id=1, source_target_pairs={{0,2},{2,4},{4,6},{6,8},{8,10},{10,12},{12,14},{14,16},{16,18},{18... | collective-permute-start | bytes 1572872 | tf_op jit(solution)/shard_map/while/body/eval_jaxpr/ppermute | solution.py:9
  79.7 3.6 copy-start.1
  85.7 1.0 copy-start.2
  86.7 11.3 %collective-permute-start = (bf16[1024,256]{1,0:T(8,128)(2,1)S(1)}, bf16[1024,256]{1,0:T(8,128)(2,1)S(1)}, u32[]{:S(2)}, u32[]{:S(2)}) collective-permute-start(bf16[1024,256]{1,0:T(8,128)(2,1)S(1)} %get-tuple-element.598), channel_id=1, source_target_pairs={{0,2},{2,4},{4,6},{6,8},{8,10},{10,12},{12,14},{14,16},{16,18},{18... | collective-permute-start | bytes 1572872 | tf_op jit(solution)/shard_map/while/body/eval_jaxpr/ppermute | solution.py:9
  100.8 3.6 copy-start.1
  106.8 1.0 copy-start.2
  107.8 11.3 %collective-permute-start = (bf16[1024,256]{1,0:T(8,128)(2,1)S(1)}, bf16[1024,256]{1,0:T(8,128)(2,1)S(1)}, u32[]{:S(2)}, u32[]{:S(2)}) collective-permute-start(bf16[1024,256]{1,0:T(8,128)(2,1)S(1)} %get-tuple-element.598), channel_id=1, source_target_pairs={{0,2},{2,4},{4,6},{6,8},{8,10},{10,12},{12,14},{14,16},{16,18},{18... | collective-permute-start | bytes 1572872 | tf_op jit(solution)/shard_map/while/body/eval_jaxpr/ppermute | solution.py:9
  121.8 3.6 copy-start.1
  127.8 1.0 copy-start.2
  128.9 11.3 %collective-permute-start = (bf16[1024,256]{1,0:T(8,128)(2,1)S(1)}, bf16[1024,256]{1,0:T(8,128)(2,1)S(1)}, u32[]{:S(2)}, u32[]{:S(2)}) collective-permute-start(bf16[1024,256]{1,0:T(8,128)(2,1)S(1)} %get-tuple-element.598), channel_id=1, source_target_pairs={{0,2},{2,4},{4,6},{6,8},{8,10},{10,12},{12,14},{14,16},{16,18},{18... | collective-permute-start | bytes 1572872 | tf_op jit(solution)/shard_map/while/body/eval_jaxpr/ppermute | solution.py:9
  142.9 3.6 copy-start.1
  148.9 1.0 copy-start.2
  149.9 11.3 %collective-permute-start = (bf16[1024,256]{1,0:T(8,128)(2,1)S(1)}, bf16[1024,256]{1,0:T(8,128)(2,1)S(1)}, u32[]{:S(2)}, u32[]{:S(2)}) collective-permute-start(bf16[1024,256]{1,0:T(8,128)(2,1)S(1)} %get-tuple-element.598), channel_id=1, source_target_pairs={{0,2},{2,4},{4,6},{6,8},{8,10},{10,12},{12,14},{14,16},{16,18},{18... | collective-permute-start | bytes 1572872 | tf_op jit(solution)/shard_map/while/body/eval_jaxpr/ppermute | solution.py:9
  164.0 3.6 copy-start.1
  170.0 1.0 copy-start.2
  171.0 11.3 %collective-permute-start = (bf16[1024,256]{1,0:T(8,128)(2,1)S(1)}, bf16[1024,256]{1,0:T(8,128)(2,1)S(1)}, u32[]{:S(2)}, u32[]{:S(2)}) collective-permute-start(bf16[1024,256]{1,0:T(8,128)(2,1)S(1)} %get-tuple-element.598), channel_id=1, source_target_pairs={{0,2},{2,4},{4,6},{6,8},{8,10},{10,12},{12,14},{14,16},{16,18},{18... | collective-permute-start | bytes 1572872 | tf_op jit(solution)/shard_map/while/body/eval_jaxpr/ppermute | solution.py:9
  185.1 3.6 copy-start.1
  191.1 1.0 copy-start.2
  193.7 26.6 %copy-start.6 = (bf16[1024,256]{1,0:T(8,128)(2,1)S(1)}, bf16[1024,256]{1,0:T(8,128)(2,1)}, u32[]{:S(2)}) copy-start(bf16[1024,256]{1,0:T(8,128)(2,1)} %param.27) | copy-start | bytes 1572868
  217.6 3.5 copy-start.7
  221.1 2.8 copy-start.3
  231.3 12.7 %collective-permute-start.1 = (f32[8,128,256]{2,0,1:T(8,128)}, f32[8,128,256]{2,0,1:T(8,128)}, u32[]{:S(2)}, u32[]{:S(2)}) collective-permute-start(f32[8,128,256]{2,0,1:T(8,128)} %get-tuple-element.632), channel_id=1, source_target_pairs={{0,30},{2,0},{4,2},{6,4},{8,6},{10,8},{12,10},{14,12},{16,14},{18,... | collective-permute-start | bytes 3145736 | tf_op jit(solution)/shard_map/while/body/eval_jaxpr/ppermute | solution.py:9
  248.6 17.2 %collective-permute-start.1 = (f32[8,128,256]{2,0,1:T(8,128)}, f32[8,128,256]{2,0,1:T(8,128)}, u32[]{:S(2)}, u32[]{:S(2)}) collective-permute-start(f32[8,128,256]{2,0,1:T(8,128)} %get-tuple-element.632), channel_id=1, source_target_pairs={{0,30},{2,0},{4,2},{6,4},{8,6},{10,8},{12,10},{14,12},{16,14},{18,... | collective-permute-start | bytes 3145736 | tf_op jit(solution)/shard_map/while/body/eval_jaxpr/ppermute | solution.py:9
  270.4 17.2 %collective-permute-start.1 = (f32[8,128,256]{2,0,1:T(8,128)}, f32[8,128,256]{2,0,1:T(8,128)}, u32[]{:S(2)}, u32[]{:S(2)}) collective-permute-start(f32[8,128,256]{2,0,1:T(8,128)} %get-tuple-element.632), channel_id=1, source_target_pairs={{0,30},{2,0},{4,2},{6,4},{8,6},{10,8},{12,10},{14,12},{16,14},{18,... | collective-permute-start | bytes 3145736 | tf_op jit(solution)/shard_map/while/body/eval_jaxpr/ppermute | solution.py:9
  292.2 17.2 %collective-permute-start.1 = (f32[8,128,256]{2,0,1:T(8,128)}, f32[8,128,256]{2,0,1:T(8,128)}, u32[]{:S(2)}, u32[]{:S(2)}) collective-permute-start(f32[8,128,256]{2,0,1:T(8,128)} %get-tuple-element.632), channel_id=1, source_target_pairs={{0,30},{2,0},{4,2},{6,4},{8,6},{10,8},{12,10},{14,12},{16,14},{18,... | collective-permute-start | bytes 3145736 | tf_op jit(solution)/shard_map/while/body/eval_jaxpr/ppermute | solution.py:9
  314.1 17.2 %collective-permute-start.1 = (f32[8,128,256]{2,0,1:T(8,128)}, f32[8,128,256]{2,0,1:T(8,128)}, u32[]{:S(2)}, u32[]{:S(2)}) collective-permute-start(f32[8,128,256]{2,0,1:T(8,128)} %get-tuple-element.632), channel_id=1, source_target_pairs={{0,30},{2,0},{4,2},{6,4},{8,6},{10,8},{12,10},{14,12},{16,14},{18,... | collective-permute-start | bytes 3145736 | tf_op jit(solution)/shard_map/while/body/eval_jaxpr/ppermute | solution.py:9
  335.9 17.2 %collective-permute-start.1 = (f32[8,128,256]{2,0,1:T(8,128)}, f32[8,128,256]{2,0,1:T(8,128)}, u32[]{:S(2)}, u32[]{:S(2)}) collective-permute-start(f32[8,128,256]{2,0,1:T(8,128)} %get-tuple-element.632), channel_id=1, source_target_pairs={{0,30},{2,0},{4,2},{6,4},{8,6},{10,8},{12,10},{14,12},{16,14},{18,... | collective-permute-start | bytes 3145736 | tf_op jit(solution)/shard_map/while/body/eval_jaxpr/ppermute | solution.py:9
  357.7 17.2 %collective-permute-start.1 = (f32[8,128,256]{2,0,1:T(8,128)}, f32[8,128,256]{2,0,1:T(8,128)}, u32[]{:S(2)}, u32[]{:S(2)}) collective-permute-start(f32[8,128,256]{2,0,1:T(8,128)} %get-tuple-element.632), channel_id=1, source_target_pairs={{0,30},{2,0},{4,2},{6,4},{8,6},{10,8},{12,10},{14,12},{16,14},{18,... | collective-permute-start | bytes 3145736 | tf_op jit(solution)/shard_map/while/body/eval_jaxpr/ppermute | solution.py:9
  379.5 14.4 %copy-start.5 = (bf16[1024,256]{1,0:T(8,128)(2,1)S(1)}, bf16[1024,256]{1,0:T(8,128)(2,1)}, u32[]{:S(2)}) copy-start(bf16[1024,256]{1,0:T(8,128)(2,1)} %param.18) | copy-start | bytes 1572868
  380.8 10.7 %collective-permute-start.3 = (bf16[8,128,256]{2,0,1:T(8,128)(2,1)S(1)}, bf16[8,128,256]{2,0,1:T(8,128)(2,1)S(1)}, u32[]{:S(2)}, u32[]{:S(2)}) collective-permute-start(bf16[8,128,256]{2,0,1:T(8,128)(2,1)S(1)} %convert_element_type.68), channel_id=1, source_target_pairs={{0,16},{2,18},{4,20},{6,22},{8,24},{10,26},{12,28},{14,30},{16,0},... | collective-permute-start | bytes 1572872 | tf_op jit(solution)/shard_map/ppermute | solution.py:9
  383.0 123.6 %all-reduce.4.cloned.1.call-start = ((), (), s32[]{:S(2)}) async-start(), calls=%async_computation | async-start | bytes 1048576 | tf_op jit(solution)/shard_map/psum | solution.py:135
  393.8 156.5 %all-gather.3.cloned.1.call-start = ((), (), s32[]{:S(2)}) async-start(), calls=%async_computation.2 | async-start | bytes 2228224 | tf_op jit(solution)/shard_map/all_gather | solution.py:117
Sparse Core Ops, SparseCore 0:
  383.1 90.3 all-reduce.5
  476.3 30.1 all-reduce.3
  509.3 41.0 all-gather.2
